TPU v7x, 32 devices: a whole 2x2x4 slice. The times are simulated.
32 devices in a mesh: seq: 4 (over z), clip: 8 (over y, x, core).
Axes of the slice: x: 2, y: 2, z: 4, core: 2. Of those that a mesh axis runs over, the one named last changes fastest.
Arguments:
- clip_features: bfloat16 [8, 4, 8, 64, 384], P('clip', None, 'seq'), may hold values from -6 to 6
- enc_weight: bfloat16 [3, 3, 3, 384, 16], replicated, may hold values from -0.0625 to 0.0625
- noise_field: float32 [8, 4, 8, 64, 16], P('clip', None, 'seq'), may hold values from -6 to 6
- flow_times: int32 [8, 2], P('clip'), may hold values from 0 to 1000, as said below
- embed_weight: bfloat16 [64, 5120], replicated, may hold values from -0.75 to 0.75
- time_weight: bfloat16 [256, 5120], replicated, may hold values from -0.375 to 0.375
- norm_gain: float32 [5120], replicated, may hold values from 0.25 to 1.75
- qkv_weight: bfloat16 [5120, 3, 3072], P('clip', None, 'seq'), may hold values from -0.078125 to 0.078125
Outputs:
- attn_out: bfloat16 [8, 512, 3072], P('clip', 'seq')
- attn_tangent: bfloat16 [8, 512, 3072], P('clip', 'seq')
Inputs may be any that keep to these rules, and one draw needn't show every extreme that they name: flow_times[c] = (index of r, index of t) with the index of r at most that of t; some clip has r index 0 and some t index 1000.
All inputs are finite; a program needn't handle non-finite values.
Results may differ from a plain program's by a relative error of at most 0.0044.
Values may be sent and summed in bfloat16 or wider, within the bound.
A program may use at most 128 MiB of HBM per device.

v0:
```python
import jax
import jax.numpy as jnp
from jax import lax
from jax.sharding import PartitionSpec as P

HD = 128
TFEAT = 256
TGRID = 1000


EPSILON = 1e-06


def padded_2(value, sides, width):
    for axis, dim in sides:
        peers, length = (lax.axis_size(axis), value.shape[dim])
        up = [(i, (i + 1) % peers) for i in range(peers - 1)]
        down = [(j, i) for i, j in up]
        last = lax.slice_in_dim(value, length - width, length, axis=dim)
        initial = lax.slice_in_dim(value, 0, width, axis=dim)
        before = lax.ppermute(last, axis, up)
        after = lax.ppermute(initial, axis, down)
        value = jnp.concatenate([before, value, after], axis=dim)
    return value


def time_features(flow_t, flow_h):
    quarter = TFEAT // 4
    freqs_omega = 8.0 * jnp.exp(-jnp.log(100.0) * jnp.arange(quarter, dtype=jnp.float32) / quarter)
    angle_t = freqs_omega * flow_t
    angle_h = freqs_omega * flow_h
    values = jnp.concatenate(
        [jnp.sin(angle_t), jnp.cos(angle_t), jnp.sin(angle_h), jnp.cos(angle_h)]
    )
    tangent = jnp.concatenate(
        [
            freqs_omega * jnp.cos(angle_t),
            -freqs_omega * jnp.sin(angle_t),
            freqs_omega * jnp.cos(angle_h),
            -freqs_omega * jnp.sin(angle_h),
        ]
    )
    return (values[None, :], tangent[None, :])


def encode(padded, enc_weight):
    frames = padded.shape[0] - 2
    rows = padded.shape[1] - 2
    columns = padded.shape[2] - 2
    latent = jnp.zeros((frames, rows, columns, enc_weight.shape[4]), jnp.float32)
    for tap_time in range(3):
        for tap_row in range(3):
            for tap_col in range(3):
                window = padded[
                    tap_time : tap_time + frames,
                    tap_row : tap_row + rows,
                    tap_col : tap_col + columns,
                ]
                latent = latent + jnp.einsum(
                    "fhwc,cz->fhwz",
                    window,
                    enc_weight[tap_time, tap_row, tap_col],
                    preferred_element_type=jnp.float32,
                )
    return latent


def patchify(field):
    frames, rows, columns, chans = field.shape
    shaped = field.reshape(frames, rows // 2, 2, columns // 2, 2, chans)
    return shaped.transpose(1, 0, 3, 2, 4, 5).reshape(-1, 4 * chans)


def embed(patches, patch_tangent, values, tangent, embed_weight, time_weight, norm_gain):
    high = lax.Precision.HIGHEST
    embed_full = embed_weight.astype(jnp.float32)
    time_full = time_weight.astype(jnp.float32)
    hidden = jnp.dot(patches, embed_full, precision=high) + jnp.dot(
        values, time_full, precision=high
    )
    hidden_t = jnp.dot(patch_tangent, embed_full, precision=high) + jnp.dot(
        tangent, time_full, precision=high
    )
    inv_rms = lax.rsqrt(jnp.mean(hidden * hidden, axis=-1, keepdims=True) + EPSILON)
    cross = jnp.mean(hidden * hidden_t, axis=-1, keepdims=True)
    normed = (hidden * inv_rms * norm_gain).astype(jnp.bfloat16)
    normed_t = (norm_gain * (hidden_t * inv_rms - hidden * inv_rms**3 * cross)).astype(jnp.bfloat16)
    return (normed, normed_t)


def attend(query, keys, vals, query_t, keys_t, vals_t):
    score_scale = query.shape[-1] ** (-0.5)
    scores = (
        jnp.einsum("hqd,hkd->hqk", query, keys, preferred_element_type=jnp.float32) * score_scale
    )
    score_t = (
        jnp.einsum("hqd,hkd->hqk", query_t, keys, preferred_element_type=jnp.float32)
        + jnp.einsum("hqd,hkd->hqk", query, keys_t, preferred_element_type=jnp.float32)
    ) * score_scale
    peak = jnp.max(scores, axis=-1, keepdims=True)
    expo = jnp.exp(scores - peak)
    probs = expo / jnp.sum(expo, axis=-1, keepdims=True)
    prob_t = probs * (score_t - jnp.sum(probs * score_t, axis=-1, keepdims=True))
    probs_b = probs.astype(jnp.bfloat16)
    prob_tb = prob_t.astype(jnp.bfloat16)
    output = jnp.einsum("hqk,hkd->hqd", probs_b, vals, preferred_element_type=jnp.float32).astype(
        jnp.bfloat16
    )
    output_t = (
        jnp.einsum("hqk,hkd->hqd", prob_tb, vals, preferred_element_type=jnp.float32)
        + jnp.einsum("hqk,hkd->hqd", probs_b, vals_t, preferred_element_type=jnp.float32)
    ).astype(jnp.bfloat16)
    return (output, output_t)


def local(
    clip_features,
    enc_weight,
    noise_field,
    flow_times,
    embed_weight,
    time_weight,
    norm_gain,
    qkv_weight,
):
    padded = padded_2(clip_features, (("seq", 2),), 1)
    padded = jnp.pad(padded[0], ((2, 0), (0, 0), (1, 1), (0, 0)))
    latent = encode(padded, enc_weight)
    start_t = flow_times[0, 0].astype(jnp.float32) / TGRID
    flow_t = flow_times[0, 1].astype(jnp.float32) / TGRID
    noise_one = noise_field[0]
    noisy = (1.0 - flow_t) * latent + flow_t * noise_one
    velocity = noise_one - latent
    patches = patchify(noisy)
    patch_t = patchify(velocity)
    values, tangent = time_features(flow_t, flow_t - start_t)
    patches, patch_t = (
        lax.all_gather(patches.astype(jnp.bfloat16), "seq", axis=0, tiled=True).astype(
            patches.dtype
        ),
        lax.all_gather(patch_t.astype(jnp.bfloat16), "seq", axis=0, tiled=True).astype(
            patch_t.dtype
        ),
    )
    normed, normed_t = embed(
        patches, patch_t, values, tangent, embed_weight, time_weight, norm_gain
    )
    tokens_all = normed.shape[0]
    piece = lax.all_gather(qkv_weight, "clip", axis=0, tiled=True)
    count = piece.shape[0]
    flat_rows = piece.reshape(count, -1)
    projected = jnp.dot(normed, flat_rows, preferred_element_type=jnp.float32)
    projected_t = jnp.dot(normed_t, flat_rows, preferred_element_type=jnp.float32)
    heads_local = qkv_weight.shape[2] // HD

    def to_heads(matrix):
        return (
            matrix.astype(jnp.bfloat16)
            .reshape(tokens_all, 3, heads_local, HD)
            .transpose(1, 2, 0, 3)
        )

    heads_p = to_heads(projected)
    heads_t = to_heads(projected_t)
    output, output_t = attend(
        heads_p[0], heads_p[1], heads_p[2], heads_t[0], heads_t[1], heads_t[2]
    )
    output = output.transpose(1, 0, 2).reshape(tokens_all, heads_local * HD)
    output_t = output_t.transpose(1, 0, 2).reshape(tokens_all, heads_local * HD)
    output, output_t = (
        lax.all_to_all(output, "seq", split_axis=0, concat_axis=1, tiled=True),
        lax.all_to_all(output_t, "seq", split_axis=0, concat_axis=1, tiled=True),
    )
    return (output[None], output_t[None])


def solution(mesh):
    placed = (
        P("clip", None, "seq", None, None),
        P(),
        P("clip", None, "seq", None, None),
        P("clip", None),
        P(),
        P(),
        P(),
        P("clip", None, "seq"),
    )
    return jax.shard_map(
        local,
        mesh=mesh,
        in_specs=placed,
        out_specs=(P("clip", "seq", None), P("clip", "seq", None)),
        check_vma=False,
    )
```

profile of v0, /device:TPU:0, one launch (start us, length us, event | category | flops | bytes accessed | tf_op | source)
XLA Modules:
  0.0 290.7 jit_solution(17552897021658005228)
XLA Ops:
  7.2 5.6 %copy.49 = bf16[640,3,768]{0,2,1:T(8,128)(2,1)} copy(bf16[640,3,768]{2,0,1:T(8,128)(2,1)} %param.15) | data formatting | bytes 5898240 | tf_op args[7]
  13.7 5.0 %collective-permute-start = (bf16[1,4,1,64,384]{4,3,2,1,0:T(8,128)(2,1)}, bf16[1,4,1,64,384]{4,3,2,1,0:T(8,128)(2,1)S(1)}, u32[]{:S(2)}, u32[]{:S(2)}) collective-permute-start(bf16[1,4,1,64,384]{4,3,2,1,0:T(8,128)(2,1)} %get-tuple-element.8), channel_id=1, source_target_pairs={{0,8},{8,16},{16,24},{1,9},{9,17},{17,25},{2,10},{10,18},{18,26},{... | collective-permute-start | bytes 589832 | tf_op jit(solution)/shard_map/ppermute | solution.py:21
  36.7 12.2 %all_gather.11 = bf16[512,64]{0,1:T(8,128)(2,1)S(1)} all-gather(bf16[128,64]{0,1:T(8,128)(2,1)S(1)} %convert_element_type.84), channel_id=1, replica_groups=mesh['seq'=4,'clip'=8] {'seq'}, dimensions={0}, use_global_device_ids=true | all-gather | bytes 81920 | tf_op jit(solution)/shard_map/all_gather | solution.py:141
  48.9 12.0 %all_gather.9 = bf16[512,64]{0,1:T(8,128)(2,1)S(1)} all-gather(bf16[128,64]{0,1:T(8,128)(2,1)S(1)} %convert_element_type.74), channel_id=1, replica_groups=mesh['seq'=4,'clip'=8] {'seq'}, dimensions={0}, use_global_device_ids=true | all-gather | bytes 81920 | tf_op jit(solution)/shard_map/all_gather | solution.py:138
  62.4 6.7 %multiply_reduce_fusion = (f32[512]{0:T(512)S(1)}, f32[512]{0:T(512)S(1)}, f32[512,5120]{1,0:T(8,128)}) fusion(f32[512,5120]{1,0:T(8,128)S(1)} %fusion.145, f32[5120]{0:T(1024)S(1)} %bitcast.289, f32[5120]{0:T(1024)S(1)} %bitcast.291, bf16[512,64]{0,1:T(8,128)(2,1)S(1)} %all_gather.11, bf16[64,5120]{1,0:T(8,128)(2,1)S(1)} %copy-done.5), kind=kOutput, calls=%fused_computation.2 | convolution fusion | flops 351271936 | bytes 21737472 | tf_op jit(solution)/shard_map/dot_general | solution.py:81
  69.2 3.6 %copy-done.2 = f32[512,5120]{1,0:T(8,128)} copy-done((f32[512,5120]{1,0:T(8,128)}, f32[512,5120]{1,0:T(8,128)S(1)}, u32[]{:S(2)}) %copy-start.2) | copy-done | bytes 10485784
  72.8 61.2 %all-gather.2.cloned.1.call-done = bf16[5120,3,768]{0,2,1:T(8,128)(2,1)} async-done(((bf16[640,3,768]{0,2,1:T(8,128)(2,1)}), bf16[5120,3,768]{0,2,1:T(8,128)(2,1)}) %all-gather.2.cloned.1.call-update) | async-done | bytes 23592976 | tf_op jit(solution)/shard_map/all_gather | solution.py:149
  134.0 20.4 %fusion.14 = bf16[512,2304]{1,0:T(8,128)(2,1)} fusion(bf16[5120,2304]{0,1:T(8,128)(2,1)} %bitcast.296, f32[512,5120]{1,0:T(8,128)} %copy-done.2, f32[5120]{0:T(1024)S(1)} %copy-done.12, f32[512]{0:T(512)S(1)} %get-tuple-element.13, f32[5120]{0:T(1024)S(1)} %bitcast.292), kind=kOutput, calls=%fused_computation.23 | convolution fusion | flops 12091260928 | bytes 36481024 | tf_op jit(solution)/shard_map/dot_general | solution.py:152
  154.4 2.8 copy.50
  157.2 2.4 copy.51
  159.7 27.6 %fusion.13 = bf16[512,2304]{1,0:T(8,128)(2,1)} fusion(bf16[5120,2304]{0,1:T(8,128)(2,1)} %bitcast.297, f32[512,5120]{1,0:T(8,128)} %get-tuple-element.16, f32[512,5120]{1,0:T(8,128)} %copy-done.2, f32[512]{0:T(512)S(1)} %broadcast_multiply_fusion, f32[512]{0:T(512)S(1)} %get-tuple-element.12, f32[5120]{0:T(1024)S(1)} %bitcast.290, f32[5120]{0:T(1024)S(1)} %copy-done.12, ...), kind=kOutput, calls=%fused_computation.22 | convolution fusion | flops 12101746688 | bytes 46991360 | tf_op jit(solution)/shard_map/dot_general | solution.py:153
  187.3 2.8 copy.57
  192.5 2.5 fusion.38
  195.1 5.3 %fusion.37 = f32[6,512,512]{1,2,0:T(8,128)} fusion(bf16[3,6,512,128]{3,2,1,0:T(8,128)(2,1)} %bitcast.283, bf16[3,6,512,128]{3,2,1,0:T(8,128)(2,1)S(1)} %bitcast.280), kind=kOutput, calls=%fused_computation.89 | convolution fusion | flops 402653184 | bytes 7864320 | tf_op jit(solution)/shard_map/hqd,hkd->hqk/dot_general | solution.py:97
  200.4 4.4 %fusion.144 = (f32[6,512]{1,0:T(8,128)S(1)}, f32[6,512,512]{1,2,0:T(8,128)}) fusion(f32[6,512,512]{1,2,0:T(8,128)S(1)} %fusion.38), kind=kOutput, calls=%fused_computation.203 | output fusion | flops 6291967 | bytes 12595200 | tf_op jit(solution)/shard_map/sub | solution.py:101
  204.8 8.4 %fusion.20 = f32[6,512,128]{2,1,0:T(8,128)} fusion(bf16[3,6,512,128]{3,2,1,0:T(8,128)(2,1)} %bitcast.284, f32[6,512]{1,0:T(8,128)S(1)} %get-tuple-element.17, f32[6,512,512]{1,2,0:T(8,128)} %copy-done.3), kind=kOutput, calls=%fused_computation.53 | convolution fusion | flops 410521088 | bytes 14954496 | tf_op jit(solution)/shard_map/hqk,hkd->hqd/dot_general | solution.py:111
  213.2 7.8 %multiply_reduce_fusion.2 = (f32[6,512]{1,0:T(8,128)S(1)}, f32[6,512,512]{1,2,0:T(8,128)}) fusion(f32[6,512,512]{1,2,0:T(8,128)} %get-tuple-element.18, f32[6,512]{1,0:T(8,128)S(1)} %get-tuple-element.17, f32[6,512,512]{1,2,0:T(8,128)} %fusion.37, bf16[3,6,512,128]{3,2,1,0:T(8,128)(2,1)} %bitcast.285, bf16[3,6,512,128]{3,2,1,0:T(8,128)(2,1)S(1)} %bitcast.281), kind=kOutput, calls=%fused_computation.6 | convolution fusion | flops 410514432 | bytes 20475904 | tf_op jit(solution)/shard_map/hqd,hkd->hqk/dot_general | solution.py:98
  221.0 10.0 %fusion.30 = bf16[512,6,128]{2,0,1:T(8,128)(2,1)S(1)} fusion(f32[6,512,128]{2,1,0:T(8,128)} %fusion.20, f32[6,512,512]{1,2,0:T(8,128)} %get-tuple-element.20, f32[6,512]{1,0:T(8,128)S(1)} %get-tuple-element.19, bf16[3,6,512,128]{3,2,1,0:T(8,128)(2,1)S(1)} %bitcast.282, f32[6,512]{1,0:T(8,128)S(1)} %get-tuple-element.17, f32[6,512,512]{1,2,0:T(8,128)} %copy-done.3), kind=kOutput, calls=%fused_computation.59 | convolution fusion | flops 414453248 | bytes 22052864 | tf_op jit(solution)/shard_map/hqk,hkd->hqd/dot_general | solution.py:110
  232.5 4.6 %all-to-all-start.1 = ((bf16[4,128,768]{1,2,0:T(8,128)(2,1)}), bf16[4,128,768]{1,2,0:T(8,128)(2,1)S(1)}, u32[]{:S(2)}, u32[]{:S(2)}) async-start(bf16[4,128,768]{1,2,0:T(8,128)(2,1)} %copy.62), calls=%async_computation.1 | async-start | bytes 1572864 | tf_op jit(solution)/shard_map/all_to_all | solution.py:172
  237.1 8.3 %fusion.27 = bf16[512,6,128]{2,0,1:T(8,128)(2,1)} fusion(bf16[3,6,512,128]{3,2,1,0:T(8,128)(2,1)} %bitcast.279, f32[6,512]{1,0:T(8,128)S(1)} %get-tuple-element.17, f32[6,512,512]{1,2,0:T(8,128)} %copy-done.3), kind=kOutput, calls=%fused_computation.58 | convolution fusion | flops 410914304 | bytes 14168064 | tf_op jit(solution)/shard_map/hqk,hkd->hqd/dot_general | solution.py:106
  247.7 2.4 all_to_all.24
  252.2 5.4 %all-to-all-done.1 = bf16[4,128,768]{1,2,0:T(8,128)(2,1)S(1)} async-done(((bf16[4,128,768]{1,2,0:T(8,128)(2,1)}), bf16[4,128,768]{1,2,0:T(8,128)(2,1)S(1)}, u32[]{:S(2)}, u32[]{:S(2)}) %all-to-all-start.1) | async-done | bytes 786464 | tf_op jit(solution)/shard_map/all_to_all | solution.py:172
  257.6 4.2 %all-to-all-start = ((bf16[4,128,768]{1,2,0:T(8,128)(2,1)}), bf16[4,128,768]{1,2,0:T(8,128)(2,1)}, u32[]{:S(2)}, u32[]{:S(2)}) async-start(bf16[4,128,768]{1,2,0:T(8,128)(2,1)} %copy.54), calls=%async_computation | async-start | bytes 1572864 | tf_op jit(solution)/shard_map/all_to_all | solution.py:171
  263.0 18.6 %all-to-all-done = bf16[4,128,768]{1,2,0:T(8,128)(2,1)} async-done(((bf16[4,128,768]{1,2,0:T(8,128)(2,1)}), bf16[4,128,768]{1,2,0:T(8,128)(2,1)}, u32[]{:S(2)}, u32[]{:S(2)}) %all-to-all-start) | async-done | bytes 786464 | tf_op jit(solution)/shard_map/all_to_all | solution.py:171
  (85 shorter events, 30.7 us)
Async XLA Ops:
  7.2 15.2 %copy-start = (bf16[256,5120]{1,0:T(8,128)(2,1)S(1)}, bf16[256,5120]{1,0:T(8,128)(2,1)}, u32[]{:S(2)}) copy-start(bf16[256,5120]{1,0:T(8,128)(2,1)} %param.13) | copy-start | bytes 7864324
  7.2 5.7 %copy-start.6 = (bf16[1,4,2,64,384]{4,3,2,1,0:T(8,128)(2,1)S(1)}, bf16[1,4,2,64,384]{4,3,2,1,0:T(8,128)(2,1)}, u32[]{:S(2)}) copy-start(bf16[1,4,2,64,384]{4,3,2,1,0:T(8,128)(2,1)} %param.8) | copy-start | bytes 1179652
  7.2 12.8 %copy-start.11 = (s32[1,2]{1,0:T(1,128)S(1)}, s32[1,2]{1,0:T(1,128)}, u32[]{:S(2)}) copy-start(s32[1,2]{1,0:T(1,128)} %param.11) | copy-start | bytes 28
  7.2 126.8 %all-gather.2.cloned.1.call-start = ((), (), s32[]{:S(2)}) async-start(), calls=%async_computation.2 | async-start | bytes 26542080 | tf_op jit(solution)/shard_map/all_gather | solution.py:149
  12.9 15.5 %copy-start.7 = (bf16[3,3,3,384,16]{3,4,2,1,0:T(8,128)(2,1)S(1)}, bf16[3,3,3,384,16]{3,4,2,1,0:T(8,128)(2,1)}, u32[]{:S(2)}) copy-start(bf16[3,3,3,384,16]{3,4,2,1,0:T(8,128)(2,1)} %param.9) | copy-start | bytes 995332
  13.7 12.2 %collective-permute-start = (bf16[1,4,1,64,384]{4,3,2,1,0:T(8,128)(2,1)}, bf16[1,4,1,64,384]{4,3,2,1,0:T(8,128)(2,1)S(1)}, u32[]{:S(2)}, u32[]{:S(2)}) collective-permute-start(bf16[1,4,1,64,384]{4,3,2,1,0:T(8,128)(2,1)} %get-tuple-element.8), channel_id=1, source_target_pairs={{0,8},{8,16},{16,24},{1,9},{9,17},{17,25},{2,10},{10,18},{18,26},{... | collective-permute-start | bytes 589832 | tf_op jit(solution)/shard_map/ppermute | solution.py:21
  18.7 8.6 %collective-permute-start.1 = (bf16[1,4,1,64,384]{4,3,2,1,0:T(8,128)(2,1)}, bf16[1,4,1,64,384]{4,3,2,1,0:T(8,128)(2,1)}, u32[]{:S(2)}, u32[]{:S(2)}) collective-permute-start(bf16[1,4,1,64,384]{4,3,2,1,0:T(8,128)(2,1)} %get-tuple-element.9), channel_id=1, source_target_pairs={{8,0},{16,8},{24,16},{9,1},{17,9},{25,17},{10,2},{18,10},{26,18},{... | collective-permute-start | bytes 589832 | tf_op jit(solution)/shard_map/ppermute | solution.py:22
  31.5 4.1 %copy-start.10 = (f32[1,4,2,64,16]{3,4,2,1,0:T(8,128)S(1)}, f32[1,4,2,64,16]{3,4,2,1,0:T(8,128)}, u32[]{:S(2)}) copy-start(f32[1,4,2,64,16]{3,4,2,1,0:T(8,128)} %param.10) | copy-start | bytes 98308
  32.0 28.9 %copy-start.5 = (bf16[64,5120]{1,0:T(8,128)(2,1)S(1)}, bf16[64,5120]{1,0:T(8,128)(2,1)}, u32[]{:S(2)}) copy-start(bf16[64,5120]{1,0:T(8,128)(2,1)} %param.12) | copy-start | bytes 1966084
  35.9 26.5 %copy-start.8 = (f32[1,5120]{1,0:T(1,128)S(1)}, f32[1,5120]{1,0:T(1,128)}, u32[]{:S(2)}) copy-start(f32[1,5120]{1,0:T(1,128)} %fusion.147) | copy-start | bytes 61444
  35.9 26.5 %copy-start.9 = (f32[1,5120]{1,0:T(1,128)S(1)}, f32[1,5120]{1,0:T(1,128)}, u32[]{:S(2)}) copy-start(f32[1,5120]{1,0:T(1,128)} %fusion.146) | copy-start | bytes 61444
  62.4 10.4 %copy-start.2 = (f32[512,5120]{1,0:T(8,128)}, f32[512,5120]{1,0:T(8,128)S(1)}, u32[]{:S(2)}) copy-start(f32[512,5120]{1,0:T(8,128)S(1)} %fusion.145) | copy-start | bytes 31457284
  62.4 71.6 %copy-start.12 = (f32[5120]{0:T(1024)S(1)}, f32[5120]{0:T(1024)}, u32[]{:S(2)}) copy-start(f32[5120]{0:T(1024)} %param.14) | copy-start | bytes 61444
  192.5 2.5 copy-start.4
  195.0 9.8 %copy-start.3 = (f32[6,512,512]{1,2,0:T(8,128)}, f32[6,512,512]{1,2,0:T(8,128)S(1)}, u32[]{:S(2)}) copy-start(f32[6,512,512]{1,2,0:T(8,128)S(1)} %fusion.38) | copy-start | bytes 18874372
  232.5 25.1 %all-to-all-start.1 = ((bf16[4,128,768]{1,2,0:T(8,128)(2,1)}), bf16[4,128,768]{1,2,0:T(8,128)(2,1)S(1)}, u32[]{:S(2)}, u32[]{:S(2)}) async-start(bf16[4,128,768]{1,2,0:T(8,128)(2,1)} %copy.62), calls=%async_computation.1 | async-start | bytes 1572864 | tf_op jit(solution)/shard_map/all_to_all | solution.py:172
  237.1 46.7 %copy-start.1 = (bf16[256,5120]{1,0:T(8,128)(2,1)S(1)}, bf16[256,5120]{1,0:T(8,128)(2,1)}, u32[]{:S(2)}) copy-start(bf16[256,5120]{1,0:T(8,128)(2,1)} %param.13) | copy-start | bytes 7864324
  257.6 23.9 %all-to-all-start = ((bf16[4,128,768]{1,2,0:T(8,128)(2,1)}), bf16[4,128,768]{1,2,0:T(8,128)(2,1)}, u32[]{:S(2)}, u32[]{:S(2)}) async-start(bf16[4,128,768]{1,2,0:T(8,128)(2,1)} %copy.54), calls=%async_computation | async-start | bytes 1572864 | tf_op jit(solution)/shard_map/all_to_all | solution.py:171
Sparse Core Ops, SparseCore 0:
  13.0 120.9 all-gather.1
where the time goes:
time: 291 us
  matrix products  110 us (38%)
  waiting for transfers between devices  86.5 us (30%)
  local copies, waits for them, and re-layouts  33.7 us (12%)
  blocking collectives  24.2 us (8%)
  between operations  15.7 us (5%)
  starting transfers between devices  15.1 us (5%)
  other arithmetic  5.93 us (2%)
    all_gather x1, waiting for transfers between devices, local(): piece = lax.all_gather(qkv_weight, 'clip', axis=0, tiled=True)  61.2 us
    dot_general x1, matrix products, local(): jnp.dot(normed_t, flat_rows, preferred_element_type=jnp.float32)  27.6 us
    dot_general x1, matrix products, local(): projected = jnp.dot(normed, flat_rows, preferred_element_type=jnp.float32)  20.4 us
    all_to_all x1, waiting for transfers between devices, local(): lax.all_to_all(output, 'seq', split_axis=0, concat_axis=1, tiled=True)  18.6 us
    unnamed x29, local copies, waits for them, and re-layouts  12.8 us
    all_gather x1, blocking collectives, local(): lax.all_gather(patch_t.astype(jnp.bfloat16), 'seq', axis=0, tiled=True)  12.2 us
    all_gather x1, blocking collectives, local(): lax.all_gather(patches.astype(jnp.bfloat16), 'seq', axis=0, tiled=True)  12 us
    dot_general x1, matrix products, attend(): jnp.einsum('hqk,hkd->hqd', prob_tb, vals, preferred_element_type=jnp.floa...  10 us
  transfers between devices with their start and end apart: 5, of which 4 were waited for; matrix products, arithmetic and copies ran while one was open for 13% of the time, Pallas kernels for 0%

commit v1 on v0

v1 whole, which is shorter than its diff:
```python
import functools

import jax
import jax.numpy as jnp
import numpy as np
from jax import lax
from jax.experimental import pallas as pl
from jax.experimental.pallas import tpu as pltpu
from jax.sharding import PartitionSpec as P

HD = 128
TFEAT = 256
TGRID = 1000
EPSILON = 1e-06
LANES = 128
F32 = jnp.float32
BF16 = jnp.bfloat16


def time_features(flow_t, flow_h):
    quarter = TFEAT // 4
    omega = 8.0 * jnp.exp(-jnp.log(100.0) * jnp.arange(quarter, dtype=F32) / quarter)
    angle_t = omega * flow_t
    angle_h = omega * flow_h
    sin_t, cos_t, sin_h, cos_h = jnp.sin(angle_t), jnp.cos(angle_t), jnp.sin(angle_h), jnp.cos(angle_h)
    values = jnp.concatenate([sin_t, cos_t, sin_h, cos_h], axis=-1)
    tangent = jnp.concatenate([omega * cos_t, -omega * sin_t, omega * cos_h, -omega * sin_h], axis=-1)
    return values, tangent


def split(value, parts):
    terms = []
    for _ in range(parts):
        term = value.astype(BF16)
        terms.append(term)
        value = value - term.astype(F32)
    return terms


def dot(a, b):
    return jnp.dot(a, b, preferred_element_type=F32)


def dot_nt(a, b):
    return lax.dot_general(a, b, (((1,), (1,)), ((), ())), preferred_element_type=F32)


def conv_part(features, weight, frames, width, chans):
    pixels = features.shape[1]
    taps = [dot_nt(weight[...], features[f]) for f in range(frames)]
    lane = lax.broadcasted_iota(jnp.int32, (chans, pixels), 1)
    column = lax.rem(lane, width)
    block = 9 * chans
    own, edge = [], []
    for f in range(frames):
        acc = taps[f][2 * block : 3 * block]
        if f >= 1:
            acc = acc + taps[f - 1][block : 2 * block]
        if f >= 2:
            acc = acc + taps[f - 2][:block]
        rows = []
        for b in range(3):
            part = [acc[(b * 3 + e) * chans : (b * 3 + e + 1) * chans] for e in range(3)]
            total = part[1]
            total = total + jnp.where(column > 0, pltpu.roll(part[0], 1, 1), 0.0)
            total = total + jnp.where(column < width - 1, pltpu.roll(part[2], pixels - 1, 1), 0.0)
            rows.append(total)
        down = pltpu.roll(rows[0], width, 1)
        up = pltpu.roll(rows[2], pixels - width, 1)
        here = rows[1] + jnp.where(lane >= width, down, 0.0)
        own.append(here + jnp.where(lane < pixels - width, up, 0.0))
        edge.append(jnp.where(lane < width, down, up))
    return jnp.concatenate(own, axis=1), jnp.concatenate(edge, axis=1)


def tokens_part(latent, noise, pick, flow_t, chans):
    tokens = pick.shape[1] // 4
    terms = split(latent, 3) + split(noise, 3)
    moved = dot(jnp.concatenate(terms, axis=0), pick)
    lat = moved[:chans] + moved[chans : 2 * chans] + moved[2 * chans : 3 * chans]
    noi = moved[3 * chans : 4 * chans] + moved[4 * chans : 5 * chans] + moved[5 * chans :]
    noisy = (1.0 - flow_t) * lat + flow_t * noi
    velocity = noi - lat
    stacked = jnp.concatenate(
        [noisy[:, k * tokens : (k + 1) * tokens] for k in range(4)]
        + [velocity[:, k * tokens : (k + 1) * tokens] for k in range(4)],
        axis=0,
    )
    flipped = stacked.T
    return flipped[:, : 4 * chans], flipped[:, 4 * chans :]


def norm_part(noisy, velocity, embed_ref, time_rows, chunk):
    tokens, patch = noisy.shape
    depth = embed_ref.shape[1]
    lhs = jnp.concatenate(
        [jnp.concatenate(split(noisy, 3), axis=1), jnp.concatenate(split(velocity, 3), axis=1)], axis=0
    )
    square = jnp.zeros((tokens, chunk), F32)
    cross = jnp.zeros((tokens, chunk), F32)
    for k in range(depth // chunk):
        piece = embed_ref[:, k * chunk : (k + 1) * chunk]
        both = dot(lhs, jnp.concatenate([piece, piece, piece], axis=0))
        hidden = both[:tokens] + time_rows[0:1, k * chunk : (k + 1) * chunk]
        hidden_t = both[tokens:] + time_rows[1:2, k * chunk : (k + 1) * chunk]
        square = square + hidden * hidden
        cross = cross + hidden * hidden_t
    mean_sq = jnp.sum(square, axis=1, keepdims=True) / depth
    mean_cr = jnp.sum(cross, axis=1, keepdims=True) / depth
    inv = lax.rsqrt(mean_sq + EPSILON)
    shift = -(inv * inv * inv) * mean_cr
    inv_hi, inv_lo = [v.astype(F32) for v in split(inv, 2)]
    sh_hi, sh_lo = [v.astype(F32) for v in split(shift, 2)]
    lane = lax.broadcasted_iota(jnp.int32, (tokens, LANES - patch), 1)

    def tail(*columns):
        out = jnp.zeros((tokens, LANES - patch), F32)
        for index, column in enumerate(columns):
            out = jnp.where(lane == index, column, out)
        return out

    rows = jnp.concatenate([noisy * inv, tail(inv_hi, inv_lo, inv_hi)], axis=1)
    rows_t = jnp.concatenate(
        [velocity * inv + noisy * shift, tail(sh_hi, sh_lo, sh_hi, inv_hi, inv_lo, inv_hi)], axis=1
    )
    return rows.astype(BF16), rows_t.astype(BF16)


MESH = pl.DeviceIdType.MESH


def front_kernel(
    dims,
    f_ref, enc_ref, noise_ref, flow_ref, feats_ref, embed_ref, ecut_ref, gcut_ref, tcut_hbm, time_hbm, w_hbm, pick_ref,
    x_out, m_out,
    tcut_ref, time_ref, w_ref, load_sem,
    feats_buf, feats_send, feats_recv,
    edge_buf, before_buf, after_buf, edge_send, edge_recv,
    e_send, e_recv, tau_send, tau_recv, e_ss, e_rs, t_ss, t_rs,
    x_buf, x_ss, x_rs,
    g_buf, tau_buf, b_ss, b_rs, bt_ss, bt_rs, a_ss, a_rs, c_ss, c_rs,
):
    frames, width, chans, peers, clips = dims
    seq, clip = lax.axis_index("seq"), lax.axis_index("clip")
    patch, depth = embed_ref.shape
    share = ecut_ref.shape[1]
    part = w_ref.shape[2]
    chunk = patch // clips
    on_seq = [{"seq": lax.rem(seq + k, peers)} for k in range(1, peers)]
    on_clip = [{"clip": lax.rem(clip + k, clips)} for k in range(1, clips)]
    mate = {"clip": clip + 1 - 2 * lax.rem(clip, 2)}

    loads = [
        pltpu.make_async_copy(src, dst, load_sem.at[k])
        for k, (src, dst) in enumerate(((w_hbm, w_ref), (tcut_hbm, tcut_ref), (time_hbm, time_ref)))
    ]
    for load in loads:
        load.start()

    barrier = pltpu.get_barrier_semaphore()
    for who in on_seq + on_clip:
        pl.semaphore_signal(barrier, inc=1, device_id=who, device_id_type=MESH)
    pl.semaphore_wait(barrier, len(on_seq) + len(on_clip))
    sent = []

    def push(src, dst, ssem, rsem, who):
        copy = pltpu.make_async_remote_copy(
            src_ref=src, dst_ref=dst, send_sem=ssem, recv_sem=rsem, device_id=who, device_id_type=MESH
        )
        copy.start()
        sent.append(copy)
        return copy

    feats_in = [
        push(feats_ref, feats_buf.at[clip], feats_send.at[k], feats_recv.at[k], who) for k, who in enumerate(on_clip)
    ]
    feats_buf[clip] = feats_ref[...]

    own, edge = conv_part(f_ref, enc_ref, frames, width, chans)
    edge_buf[...] = edge

    def edge_copy(dst, k, step):
        return pltpu.make_async_remote_copy(
            src_ref=edge_buf, dst_ref=dst, send_sem=edge_send.at[k], recv_sem=edge_recv.at[k],
            device_id={"seq": lax.rem(seq + peers + step, peers)}, device_id_type=MESH,
        )

    to_next, to_last = edge_copy(before_buf, 0, 1), edge_copy(after_buf, 1, -1)

    @pl.when(seq < peers - 1)
    def _():
        to_next.start()

    @pl.when(seq > 0)
    def _():
        to_last.start()

    @pl.when(seq == 0)
    def _():
        before_buf[...] = jnp.zeros_like(before_buf)

    @pl.when(seq == peers - 1)
    def _():
        after_buf[...] = jnp.zeros_like(after_buf)

    gain = gcut_ref[...]
    left = jnp.concatenate(split(ecut_ref[...].astype(F32) * gain, 2), axis=0)
    loads[0].wait()
    for i in range(3):
        both = dot(left, w_ref[i])
        both = both[:patch] + both[patch:]
        for c in range(clips):
            e_send[c, :, i * part : (i + 1) * part] = both[c * chunk : (c + 1) * chunk]
    e_in = [
        push(e_send.at[lax.rem(clip + k + 1, clips)], e_recv.at[k], e_ss.at[k], e_rs.at[k], who)
        for k, who in enumerate(on_clip)
    ]
    for copy in feats_in:
        copy.wait_recv()
    loads[1].wait()
    feats = feats_buf[...].reshape(clips * 8, feats_buf.shape[2])
    both = dot(jnp.concatenate(split(feats, 2), axis=0), tcut_ref[...])
    left = jnp.concatenate(split((both[: clips * 8] + both[clips * 8 :]) * gain, 2), axis=0)
    for i in range(3):
        both = dot(left, w_ref[i])
        both = both[: clips * 8] + both[clips * 8 :]
        for c in range(clips):
            tau_send[c, :, i * part : (i + 1) * part] = both[c * 8 : c * 8 + 2]
    tau_in = [
        push(tau_send.at[lax.rem(clip + k + 1, clips)], tau_recv.at[k], t_ss.at[k], t_rs.at[k], who)
        for k, who in enumerate(on_clip)
    ]

    loads[2].wait()
    mine = jnp.concatenate(split(feats_ref[...], 2), axis=0)
    times = dot(mine, time_ref[...])
    times = times[:8] + times[8:]

    @pl.when(seq > 0)
    def _():
        to_next.wait_recv()

    @pl.when(seq < peers - 1)
    def _():
        to_last.wait_recv()

    pixels = f_ref.shape[1]
    lane = lax.rem(lax.broadcasted_iota(jnp.int32, own.shape, 1), pixels)
    latent = own + jnp.where(lane < width, before_buf[...], 0.0)
    latent = latent + jnp.where(lane >= pixels - width, after_buf[...], 0.0)
    noise = jnp.concatenate(
        [noise_ref[f, r] for f in range(frames) for r in range(noise_ref.shape[1])], axis=1
    )
    noisy, velocity = tokens_part(latent, noise, pick_ref[...], flow_ref[...], chans)
    rows, rows_t = norm_part(noisy, velocity, embed_ref, times, 512)
    x_buf[seq, 0] = rows
    x_buf[seq, 1] = rows_t
    x_in = [push(x_buf.at[seq], x_buf.at[seq], x_ss.at[k], x_rs.at[k], who) for k, who in enumerate(on_seq)]

    for copy in e_in:
        copy.wait_recv()
    total = e_send[clip]
    for k in range(clips - 1):
        total = total + e_recv[k]
    g_buf[clip, seq] = total.astype(BF16)
    b_in = [
        push(g_buf.at[clip, seq], g_buf.at[clip, seq], b_ss.at[k], b_rs.at[k], who) for k, who in enumerate(on_seq)
    ]
    for copy in tau_in:
        copy.wait_recv()
    total = tau_send[clip]
    for k in range(clips - 1):
        total = total + tau_recv[k]
    tau_buf[seq] = total
    bt_in = [
        push(tau_buf.at[seq], tau_buf.at[seq], bt_ss.at[k], bt_rs.at[k], who) for k, who in enumerate(on_seq)
    ]
    for copy in b_in:
        copy.wait_recv()
    c_in = [push(g_buf.at[clip], g_buf.at[clip], c_ss.at[0], c_rs.at[0], mate)]
    a_in = [
        push(g_buf.at[clip], g_buf.at[clip], a_ss.at[k], a_rs.at[k], on_clip[2 * k + 1])
        for k in range(clips // 2 - 1)
    ]
    for k, copy in enumerate(a_in):
        copy.wait_recv()
        src = lax.rem(clip + clips - 2 * (k + 1), clips)
        c_in.append(push(g_buf.at[src], g_buf.at[src], c_ss.at[k + 1], c_rs.at[k + 1], mate))
    for copy in bt_in + x_in + c_in:
        copy.wait_recv()
    for p in range(peers):
        x_out[0, p * x_buf.shape[2] : (p + 1) * x_buf.shape[2]] = x_buf[p, 0]
        x_out[1, p * x_buf.shape[2] : (p + 1) * x_buf.shape[2]] = x_buf[p, 1]
        for c in range(clips):
            m_out[p, c * chunk : (c + 1) * chunk] = g_buf[c, p]
        hi = tau_buf[p].astype(BF16).astype(F32)
        lo = tau_buf[p] - hi
        extra = [hi[0:1], hi[0:1], lo[0:1], hi[1:2], hi[1:2], lo[1:2]]
        row = lax.broadcasted_iota(jnp.int32, (LANES - patch, 3 * part), 0)
        tail = jnp.zeros((LANES - patch, 3 * part), F32)
        for index, value in enumerate(extra):
            tail = jnp.where(row == index, value, tail)
        m_out[p, patch:] = tail.astype(BF16)
    for copy in sent:
        copy.wait_send()

    @pl.when(seq < peers - 1)
    def _():
        to_next.wait_send()

    @pl.when(seq > 0)
    def _():
        to_last.wait_send()


def attend_kernel(per, x_ref, xt_ref, xo_ref, xto_ref, q_ref, k_ref, v_ref, out_ref, out_t_ref):
    scale = HD ** (-0.5)
    wq, wk, wv = q_ref[0], k_ref[0], v_ref[0]

    def project(rows_ref, weight):
        return dot(rows_ref[...], weight).astype(BF16)

    keys, keys_t = project(x_ref, wk), project(xt_ref, wk)
    vals, vals_t = project(x_ref, wv), project(xt_ref, wv)
    query, query_t = project(xo_ref, wq), project(xto_ref, wq)
    for h in range(per):
        at = slice(h * HD, (h + 1) * HD)
        q, qt, k, kt, v, vt = (m[:, at] for m in (query, query_t, keys, keys_t, vals, vals_t))
        scores = dot_nt(q, k) * scale
        score_t = dot_nt(jnp.concatenate([qt, q], axis=1), jnp.concatenate([k, kt], axis=1)) * scale
        expo = jnp.exp(scores - jnp.max(scores, axis=1, keepdims=True))
        probs = expo * (1.0 / jnp.sum(expo, axis=1, keepdims=True))
        prob_t = probs * (score_t - jnp.sum(probs * score_t, axis=1, keepdims=True))
        pb, ptb = probs.astype(BF16), prob_t.astype(BF16)
        out_ref[:, at] = dot(pb, v).astype(BF16)
        out_t_ref[:, at] = (dot(ptb, v) + dot(pb, vt)).astype(BF16)


VMEM = pl.BlockSpec(memory_space=pltpu.VMEM)


def attend(rows, rows_t, own, own_t, weights, inner):
    peers, depth, width = weights.shape
    part = width // 3
    per = 2 if (part // HD) % 2 == 0 else 1
    block = per * HD
    count = part // block
    tokens, total = own.shape[0], rows.shape[0]
    whole = lambda n: pl.BlockSpec((n, LANES), lambda i: (0, 0))
    spec = lambda g: pl.BlockSpec((1, depth, block), lambda i: (i // count, 0, g * count + i % count))
    out = pl.BlockSpec((tokens, block), lambda i: (0, i))
    shape = jax.ShapeDtypeStruct((tokens, inner), BF16)
    return pl.pallas_call(
        functools.partial(attend_kernel, per),
        grid=(peers * count,),
        out_shape=(shape, shape),
        in_specs=[whole(total), whole(total), whole(tokens), whole(tokens), spec(0), spec(1), spec(2)],
        out_specs=(out, out),
        name="attend",
    )(rows, rows_t, own, own_t, weights, weights, weights)


def local(clip_features, enc_weight, noise_field, flow_times, embed_weight, time_weight, norm_gain, qkv_weight):
    _, frames, rows, width, depth_c = clip_features.shape
    chans = enc_weight.shape[4]
    patch, depth = embed_weight.shape
    peers, clips = lax.axis_size("seq"), lax.axis_size("clip")
    share = qkv_weight.shape[0]
    part = qkv_weight.shape[2]
    pixels = rows * width
    tokens = frames * pixels // 4

    me = lax.axis_index("clip")
    gain = lax.dynamic_slice_in_dim(norm_gain, me * share, share, 0)[None, :]
    embed_cut = lax.dynamic_slice_in_dim(embed_weight, me * share, share, 1)
    time_cut = lax.dynamic_slice_in_dim(time_weight, me * share, share, 1)
    weight = qkv_weight.transpose(1, 0, 2)
    flow = flow_times.astype(F32) / TGRID
    values, tangent = time_features(flow[:, 1:2], flow[:, 1:2] - flow[:, 0:1])
    feats = jnp.concatenate([values, tangent, jnp.zeros((6, values.shape[1]), F32)], axis=0)
    features = clip_features.reshape(frames, pixels, depth_c)
    enc = enc_weight.transpose(0, 1, 2, 4, 3).reshape(27 * chans, depth_c)
    noise = noise_field[0].transpose(0, 1, 3, 2)
    i, f, j = np.meshgrid(np.arange(rows // 2), np.arange(frames), np.arange(width // 2), indexing="ij")
    source = np.stack(
        [((f * rows + 2 * i + p) * width + 2 * j + q).reshape(-1) for p in range(2) for q in range(2)]
    ).reshape(1, -1)
    pick = (jnp.arange(frames * pixels, dtype=jnp.int32)[:, None] == source.astype(np.int32)).astype(BF16)
    chunk = patch // clips
    dma = pltpu.SemaphoreType.DMA
    anywhere = pl.BlockSpec(memory_space=pl.ANY)
    edge = pltpu.VMEM((chans, frames * pixels), F32)
    gathered, weights = pl.pallas_call(
        functools.partial(front_kernel, (frames, width, chans, peers, clips)),
        out_shape=(
            jax.ShapeDtypeStruct((2, peers * tokens, LANES), BF16),
            jax.ShapeDtypeStruct((peers, LANES, 3 * part), BF16),
        ),
        in_specs=[VMEM] * 8 + [anywhere] * 3 + [VMEM],
        out_specs=(VMEM, VMEM),
        scratch_shapes=[
            pltpu.VMEM(time_cut.shape, BF16), pltpu.VMEM(time_weight.shape, BF16), pltpu.VMEM(weight.shape, BF16), dma((3,)),
            pltpu.VMEM((clips, 8, feats.shape[1]), F32), dma((clips - 1,)), dma((clips - 1,)),
            edge, edge, edge, dma((2,)), dma((2,)),
            pltpu.VMEM((clips, chunk, 3 * part), F32), pltpu.VMEM((clips - 1, chunk, 3 * part), F32),
            pltpu.VMEM((clips, 2, 3 * part), F32), pltpu.VMEM((clips - 1, 2, 3 * part), F32),
            dma((clips - 1,)), dma((clips - 1,)), dma((clips - 1,)), dma((clips - 1,)),
            pltpu.VMEM((peers, 2, tokens, LANES), BF16), dma((peers - 1,)), dma((peers - 1,)),
            pltpu.VMEM((clips, peers, chunk, 3 * part), BF16), pltpu.VMEM((peers, 2, 3 * part), F32),
            dma((peers - 1,)), dma((peers - 1,)), dma((peers - 1,)), dma((peers - 1,)),
            dma((clips // 2,)), dma((clips // 2,)), dma((clips // 2,)), dma((clips // 2,)),
        ],
        compiler_params=pltpu.CompilerParams(collective_id=0, has_side_effects=True),
        name="front",
    )(features, enc, noise, flow[:, 1:2], feats, embed_weight, embed_cut, gain, time_cut, time_weight, weight, pick)
    at = lax.axis_index("seq") * tokens
    x_own = lax.dynamic_slice_in_dim(gathered[0], at, tokens, 0)
    xt_own = lax.dynamic_slice_in_dim(gathered[1], at, tokens, 0)
    output, output_t = attend(gathered[0], gathered[1], x_own, xt_own, weights, peers * part)
    return output[None], output_t[None]


def solution(mesh):
    placed = (
        P("clip", None, "seq", None, None),
        P(),
        P("clip", None, "seq", None, None),
        P("clip", None),
        P(),
        P(),
        P(),
        P("clip", None, "seq"),
    )
    return jax.shard_map(
        local,
        mesh=mesh,
        in_specs=placed,
        out_specs=(P("clip", "seq", None), P("clip", "seq", None)),
        check_vma=False,
    )
```

time: 291 us -> 70.6 us (0.24)
  matrix products: 110 us -> 0 us
  waiting for transfers between devices: 86.5 us -> 0 us
  Pallas kernels: 0 us -> 56.1 us
  local copies, waits for them, and re-layouts: 33.7 us -> 8.23 us
  blocking collectives: 24.2 us -> 0 us
  starting transfers between devices: 15.1 us -> 0 us
  between operations: 15.7 us -> 2.56 us
    dot_general x39 -> x0, matrix products: 110 us -> none  [the longest x1 27.6 us: local(): jnp.dot(normed_t, flat_rows, preferred_element_type=jnp.float32)]
    all_gather x1 -> x0, waiting for transfers between devices: 61.2 us -> none  [local(): piece = lax.all_gather(qkv_weight, 'clip', axis=0, tiled=True)]
    pallas_call x0 -> x2, Pallas kernels: none -> 56.1 us  [the longest x1 35.7 us: local(): pl.pallas_call(functools.partial(front_kernel, (frames, width, chans, pee...]
    all_gather x2 -> x0, blocking collectives: 24.2 us -> none  [the longest x1 12.2 us: local(): lax.all_gather(patch_t.astype(jnp.bfloat16), 'seq', axis=0, tiled=True)]
    all_to_all x2 -> x0, waiting for transfers between devices: 23.9 us -> none  [the longest x1 18.6 us: local(): lax.all_to_all(output, 'seq', split_axis=0, concat_axis=1, tiled=True)]
    unnamed x29 -> x0, local copies, waits for them, and re-layouts: 12.8 us -> none
    convert_element_type x10 -> x0, local copies, waits for them, and re-layouts: 8.95 us -> none  [the longest x2 5.67 us: to_heads(): matrix.astype(jnp.bfloat16).reshape(tokens_all, 3, heads_local, HD)]
    all_to_all x2 -> x0, starting transfers between devices: 8.82 us -> none  [the longest x1 4.63 us: local(): lax.all_to_all(output_t, 'seq', split_axis=0, concat_axis=1, tiled=True)]
  transfers between devices with their start and end apart: 5 -> 0, of which waited for: 4 -> 0; matrix products, arithmetic and copies ran while one was open for 13% -> 0% of each run, Pallas kernels for 0% -> 0%
where the time goes in v1:
time: 70.6 us; the launch traced here: 70 us
  Pallas kernels  56.1 us (79%)
  local copies, waits for them, and re-layouts  8.23 us (12%)
  other arithmetic  3.16 us (4%)
  between operations  2.56 us (4%)
    pallas_call x1, Pallas kernels, local(): pl.pallas_call(functools.partial(front_kernel, (frames, width, chans, pee...  35.7 us
    pallas_call x1, Pallas kernels, attend(): pl.pallas_call(functools.partial(attend_kernel, per), grid=(peers * count...  20.4 us
    slice x1, local copies, waits for them, and re-layouts, local(): gathered[1]  1.74 us
    dynamic_slice x1, local copies, waits for them, and re-layouts, local(): time_cut = lax.dynamic_slice_in_dim(time_weight, me * share, share, 1)  1.72 us
    convert_element_type x1, other arithmetic, local(): (jnp.arange(frames * pixels, dtype=jnp.int32)[:, None] == source.astype(n...  1.61 us
    dynamic_slice x1, local copies, waits for them, and re-layouts, local(): embed_cut = lax.dynamic_slice_in_dim(embed_weight, me * share, share, 1)  1.52 us

profile of v1, /device:TPU:0, one launch (start us, length us, event | category | flops | bytes accessed | tf_op | source)
XLA Modules:
  0.0 70.0 jit_solution(17526177382083784411)
XLA Ops:
  0.6 0.7 convert_multiply_fusion
  1.3 0.1 pad.8.clone
  1.4 0.6 fusion.4
  3.9 0.1 negate_multiply_fusion
  3.9 0.1 multiply_sine_fusion
  4.0 0.1 negate_multiply_fusion.1
  4.0 0.1 multiply_sine_fusion.1
  4.1 0.7 maximum_maximum_fusion.feats_ref
  4.8 0.8 %dynamic_slice.20 = f32[640]{0:T(1024)S(1)} dynamic-slice(f32[5120]{0:T(1024)} %param.15, s32[]{:T(128)S(6)} %select_n.4), dynamic_slice_sizes={640} | dynamic-slice | bytes 5124 | tf_op jit(solution)/shard_map/dynamic_slice | solution.py:374
  5.5 0.6 broadcast_in_dim.9.gcut_ref
  6.1 1.5 %constant_dynamic-slice_fusion.1.ecut_ref = bf16[64,640]{1,0:T(8,128)(2,1)} fusion(bf16[64,5120]{1,0:T(8,128)(2,1)} %embed_ref.1, s32[]{:T(128)S(6)} %select_n.4), kind=kLoop, calls=%fused_computation.6 | loop fusion | bytes 163844 | tf_op jit(solution)/shard_map/dynamic_slice | solution.py:375
  7.6 1.7 %constant_dynamic-slice_fusion.tcut_hbm = bf16[256,640]{1,0:T(8,128)(2,1)} fusion(bf16[256,5120]{1,0:T(8,128)(2,1)} %time_hbm.1, s32[]{:T(128)S(6)} %select_n.4), kind=kLoop, calls=%fused_computation.5 | loop fusion | bytes 655364 | tf_op jit(solution)/shard_map/dynamic_slice | solution.py:376
  9.4 1.6 %fusion.pick_ref = bf16[512,512]{1,0:T(8,128)(2,1)} fusion(s32[512]{0:T(512)} %constant.48), kind=kLoop, calls=%fused_computation.1 | loop fusion | flops 524288 | bytes 526336 | tf_op jit(solution)/shard_map/convert_element_type | solution.py:388
  11.0 35.7 %front.1 = (bf16[2,512,128]{2,1,0:T(8,128)(2,1)}, bf16[4,128,2304]{2,1,0:T(8,128)(2,1)}) custom-call(bf16[4,128,384]{2,1,0:T(8,128)(2,1)} %bitcast.21, bf16[432,384]{1,0:T(8,128)(2,1)} %bitcast.22, f32[4,2,16,64]{3,2,1,0:T(8,128)} %bitcast.23, f32[1,1]{1,0:T(1,128)} %get-tuple-element.15.flow_ref, f32[8,256]{1,0:T(8,128)} %maximum_maximum_fusion.feats_ref, ...), custom_call_target="tpu_custom_call" | custom-call | tf_op jit(solution)/shard_map/front/pallas_call | solution.py:393
  46.6 1.7 %fusion.3 = (bf16[1,512,128]{2,1,0:T(8,128)(2,1)S(1)}, bf16[512,128]{1,0:T(8,128)(2,1)}, bf16[512,128]{1,0:T(8,128)(2,1)}, bf16[1,512,128]{2,1,0:T(8,128)(2,1)S(1)}) fusion(bf16[2,512,128]{2,1,0:T(8,128)(2,1)} %get-tuple-element.6), kind=kLoop, calls=%fused_computation.20 | loop fusion | bytes 786432 | tf_op jit(solution)/shard_map/slice | solution.py:419
  48.4 0.6 dynamic-slice_bitcast_fusion.xto_ref
  49.0 0.6 dynamic-slice_bitcast_fusion.1.xo_ref
  49.6 20.4 %attend.1 = (bf16[128,3072]{1,0:T(8,128)(2,1)}, bf16[128,3072]{1,0:T(8,128)(2,1)}) custom-call(bf16[512,128]{1,0:T(8,128)(2,1)} %get-tuple-element.11.x_ref, bf16[512,128]{1,0:T(8,128)(2,1)} %get-tuple-element.12.xt_ref, bf16[128,128]{1,0:T(8,128)(2,1)} %dynamic-slice_bitcast_fusion.1.xo_ref, bf16[128,128]{1,0:T(8,128)(2,1)} %dynamic-slice_bitcast_fusion.xto_ref, ...), custom_call_target="tpu_custom_call" | custom-call | tf_op jit(solution)/shard_map/attend/pallas_call | solution.py:353
  (1 shorter events, 0.0 us)

commit v2 on v1

--- a/solution.py
+++ b/solution.py
@@ -15,17 +15,6 @@
 LANES = 128
 F32 = jnp.float32
 BF16 = jnp.bfloat16
-
-
-def time_features(flow_t, flow_h):
-    quarter = TFEAT // 4
-    omega = 8.0 * jnp.exp(-jnp.log(100.0) * jnp.arange(quarter, dtype=F32) / quarter)
-    angle_t = omega * flow_t
-    angle_h = omega * flow_h
-    sin_t, cos_t, sin_h, cos_h = jnp.sin(angle_t), jnp.cos(angle_t), jnp.sin(angle_h), jnp.cos(angle_h)
-    values = jnp.concatenate([sin_t, cos_t, sin_h, cos_h], axis=-1)
-    tangent = jnp.concatenate([omega * cos_t, -omega * sin_t, omega * cos_h, -omega * sin_h], axis=-1)
-    return values, tangent
 
 
 def split(value, parts):
@@ -131,9 +120,9 @@
 
 def front_kernel(
     dims,
-    f_ref, enc_ref, noise_ref, flow_ref, feats_ref, embed_ref, ecut_ref, gcut_ref, tcut_hbm, time_hbm, w_hbm, pick_ref,
-    x_out, m_out,
-    tcut_ref, time_ref, w_ref, load_sem,
+    flow_ref, source_ref, w_hbm, ecut_hbm, gcut_hbm, tcut_hbm, f_hbm, enc_hbm, time_hbm, noise_hbm, embed_hbm,
+    x_out, xt_out, x_own, xt_own, m_out,
+    w_ref, ecut_ref, gcut_ref, tcut_ref, f_ref, enc_ref, time_ref, noise_ref, embed_ref, load_sem, feats_ref,
     feats_buf, feats_send, feats_recv,
     edge_buf, before_buf, after_buf, edge_send, edge_recv,
     e_send, e_recv, tau_send, tau_recv, e_ss, e_rs, t_ss, t_rs,
@@ -150,12 +139,32 @@
     on_clip = [{"clip": lax.rem(clip + k, clips)} for k in range(1, clips)]
     mate = {"clip": clip + 1 - 2 * lax.rem(clip, 2)}
 
-    loads = [
-        pltpu.make_async_copy(src, dst, load_sem.at[k])
-        for k, (src, dst) in enumerate(((w_hbm, w_ref), (tcut_hbm, tcut_ref), (time_hbm, time_ref)))
-    ]
+    def cut(ref):
+        if ref.shape[-1] == share:
+            return ref
+        return ref.at[:, pl.ds(pl.multiple_of(clip * share, share), share)]
+
+    pairs = (
+        (w_hbm, w_ref), (cut(ecut_hbm), ecut_ref), (cut(gcut_hbm), gcut_ref), (cut(tcut_hbm), tcut_ref),
+        (f_hbm, f_ref), (enc_hbm, enc_ref), (time_hbm, time_ref), (noise_hbm, noise_ref), (embed_hbm, embed_ref),
+    )
+    loads = [pltpu.make_async_copy(src, dst, load_sem.at[k]) for k, (src, dst) in enumerate(pairs)]
     for load in loads:
         load.start()
+    flow_r = flow_ref[0, 0].astype(F32) / TGRID
+    flow_t = flow_ref[0, 1].astype(F32) / TGRID
+    quarter = TFEAT // 4
+    order = lax.broadcasted_iota(jnp.int32, (8, TFEAT), 1)
+    line = lax.broadcasted_iota(jnp.int32, (8, TFEAT), 0)
+    omega = 8.0 * jnp.exp(-np.float32(np.log(100.0)) * lax.rem(order, quarter).astype(F32) / quarter)
+    angle = omega * jnp.where(order < 2 * quarter, flow_t, flow_t - flow_r)
+    sine, cosine = jnp.sin(angle), jnp.cos(angle)
+    first = lax.rem(order // quarter, 2) == 0
+    feats_ref[...] = jnp.where(
+        line == 0,
+        jnp.where(first, sine, cosine),
+        jnp.where(line == 1, jnp.where(first, omega * cosine, -omega * sine), 0.0),
+    )
 
     barrier = pltpu.get_barrier_semaphore()
     for who in on_seq + on_clip:
@@ -176,33 +185,8 @@
     ]
     feats_buf[clip] = feats_ref[...]
 
-    own, edge = conv_part(f_ref, enc_ref, frames, width, chans)
-    edge_buf[...] = edge
-
-    def edge_copy(dst, k, step):
-        return pltpu.make_async_remote_copy(
-            src_ref=edge_buf, dst_ref=dst, send_sem=edge_send.at[k], recv_sem=edge_recv.at[k],
-            device_id={"seq": lax.rem(seq + peers + step, peers)}, device_id_type=MESH,
-        )
-
-    to_next, to_last = edge_copy(before_buf, 0, 1), edge_copy(after_buf, 1, -1)
-
-    @pl.when(seq < peers - 1)
-    def _():
-        to_next.start()
-
-    @pl.when(seq > 0)
-    def _():
-        to_last.start()
-
-    @pl.when(seq == 0)
-    def _():
-        before_buf[...] = jnp.zeros_like(before_buf)
-
-    @pl.when(seq == peers - 1)
-    def _():
-        after_buf[...] = jnp.zeros_like(after_buf)
-
+    loads[1].wait()
+    loads[2].wait()
     gain = gcut_ref[...]
     left = jnp.concatenate(split(ecut_ref[...].astype(F32) * gain, 2), axis=0)
     loads[0].wait()
@@ -217,7 +201,7 @@
     ]
     for copy in feats_in:
         copy.wait_recv()
-    loads[1].wait()
+    loads[3].wait()
     feats = feats_buf[...].reshape(clips * 8, feats_buf.shape[2])
     both = dot(jnp.concatenate(split(feats, 2), axis=0), tcut_ref[...])
     left = jnp.concatenate(split((both[: clips * 8] + both[clips * 8 :]) * gain, 2), axis=0)
@@ -231,31 +215,39 @@
         for k, who in enumerate(on_clip)
     ]
 
-    loads[2].wait()
+    loads[4].wait()
+    loads[5].wait()
+    own, edge = conv_part(f_ref, enc_ref, frames, width, chans)
+    edge_buf[...] = edge
+
+    def edge_copy(dst, k, step):
+        return pltpu.make_async_remote_copy(
+            src_ref=edge_buf, dst_ref=dst, send_sem=edge_send.at[k], recv_sem=edge_recv.at[k],
+            device_id={"seq": lax.rem(seq + peers + step, peers)}, device_id_type=MESH,
+        )
+
+    to_next, to_last = edge_copy(before_buf, 0, 1), edge_copy(after_buf, 1, -1)
+
+    @pl.when(seq < peers - 1)
+    def _():
+        to_next.start()
+
+    @pl.when(seq > 0)
+    def _():
+        to_last.start()
+
+    @pl.when(seq == 0)
+    def _():
+        before_buf[...] = jnp.zeros_like(before_buf)
+
+    @pl.when(seq == peers - 1)
+    def _():
+        after_buf[...] = jnp.zeros_like(after_buf)
+
+    loads[6].wait()
     mine = jnp.concatenate(split(feats_ref[...], 2), axis=0)
     times = dot(mine, time_ref[...])
     times = times[:8] + times[8:]
-
-    @pl.when(seq > 0)
-    def _():
-        to_next.wait_recv()
-
-    @pl.when(seq < peers - 1)
-    def _():
-        to_last.wait_recv()
-
-    pixels = f_ref.shape[1]
-    lane = lax.rem(lax.broadcasted_iota(jnp.int32, own.shape, 1), pixels)
-    latent = own + jnp.where(lane < width, before_buf[...], 0.0)
-    latent = latent + jnp.where(lane >= pixels - width, after_buf[...], 0.0)
-    noise = jnp.concatenate(
-        [noise_ref[f, r] for f in range(frames) for r in range(noise_ref.shape[1])], axis=1
-    )
-    noisy, velocity = tokens_part(latent, noise, pick_ref[...], flow_ref[...], chans)
-    rows, rows_t = norm_part(noisy, velocity, embed_ref, times, 512)
-    x_buf[seq, 0] = rows
-    x_buf[seq, 1] = rows_t
-    x_in = [push(x_buf.at[seq], x_buf.at[seq], x_ss.at[k], x_rs.at[k], who) for k, who in enumerate(on_seq)]
 
     for copy in e_in:
         copy.wait_recv()
@@ -275,6 +267,31 @@
     bt_in = [
         push(tau_buf.at[seq], tau_buf.at[seq], bt_ss.at[k], bt_rs.at[k], who) for k, who in enumerate(on_seq)
     ]
+    @pl.when(seq > 0)
+    def _():
+        to_next.wait_recv()
+
+    @pl.when(seq < peers - 1)
+    def _():
+        to_last.wait_recv()
+
+    pixels = f_ref.shape[1]
+    lane = lax.rem(lax.broadcasted_iota(jnp.int32, own.shape, 1), pixels)
+    latent = own + jnp.where(lane < width, before_buf[...], 0.0)
+    latent = latent + jnp.where(lane >= pixels - width, after_buf[...], 0.0)
+    loads[7].wait()
+    loads[8].wait()
+    noise = jnp.concatenate(
+        [noise_ref[f, r] for f in range(frames) for r in range(noise_ref.shape[1])], axis=1
+    )
+    places = lax.broadcasted_iota(jnp.int32, (own.shape[1], source_ref.shape[1]), 0)
+    pick = (places == source_ref[...]).astype(F32).astype(BF16)
+    noisy, velocity = tokens_part(latent, noise, pick, flow_t, chans)
+    rows, rows_t = norm_part(noisy, velocity, embed_ref, times, 512)
+    x_buf[seq, 0] = rows
+    x_buf[seq, 1] = rows_t
+    x_in = [push(x_buf.at[seq], x_buf.at[seq], x_ss.at[k], x_rs.at[k], who) for k, who in enumerate(on_seq)]
+
     for copy in b_in:
         copy.wait_recv()
     c_in = [push(g_buf.at[clip], g_buf.at[clip], c_ss.at[0], c_rs.at[0], mate)]
@@ -288,9 +305,12 @@
         c_in.append(push(g_buf.at[src], g_buf.at[src], c_ss.at[k + 1], c_rs.at[k + 1], mate))
     for copy in bt_in + x_in + c_in:
         copy.wait_recv()
+    x_own[...] = x_buf[seq, 0]
+    xt_own[...] = x_buf[seq, 1]
+    tokens = x_buf.shape[2]
     for p in range(peers):
-        x_out[0, p * x_buf.shape[2] : (p + 1) * x_buf.shape[2]] = x_buf[p, 0]
-        x_out[1, p * x_buf.shape[2] : (p + 1) * x_buf.shape[2]] = x_buf[p, 1]
+        x_out[p * tokens : (p + 1) * tokens] = x_buf[p, 0]
+        xt_out[p * tokens : (p + 1) * tokens] = x_buf[p, 1]
         for c in range(clips):
             m_out[p, c * chunk : (c + 1) * chunk] = g_buf[c, p]
         hi = tau_buf[p].astype(BF16).astype(F32)
@@ -326,14 +346,14 @@
     for h in range(per):
         at = slice(h * HD, (h + 1) * HD)
         q, qt, k, kt, v, vt = (m[:, at] for m in (query, query_t, keys, keys_t, vals, vals_t))
-        scores = dot_nt(q, k) * scale
-        score_t = dot_nt(jnp.concatenate([qt, q], axis=1), jnp.concatenate([k, kt], axis=1)) * scale
-        expo = jnp.exp(scores - jnp.max(scores, axis=1, keepdims=True))
-        probs = expo * (1.0 / jnp.sum(expo, axis=1, keepdims=True))
-        prob_t = probs * (score_t - jnp.sum(probs * score_t, axis=1, keepdims=True))
-        pb, ptb = probs.astype(BF16), prob_t.astype(BF16)
-        out_ref[:, at] = dot(pb, v).astype(BF16)
-        out_t_ref[:, at] = (dot(ptb, v) + dot(pb, vt)).astype(BF16)
+        scores = dot_nt(q, k)
+        score_t = dot_nt(jnp.concatenate([qt, q], axis=1), jnp.concatenate([k, kt], axis=1))
+        expo = jnp.exp((scores - jnp.max(scores, axis=1, keepdims=True)) * scale)
+        inv = 1.0 / jnp.sum(expo, axis=1, keepdims=True)
+        mean = jnp.sum(expo * score_t, axis=1, keepdims=True) * inv
+        eb, etb = expo.astype(BF16), (expo * (score_t - mean)).astype(BF16)
+        out_ref[:, at] = (dot(eb, v) * inv).astype(BF16)
+        out_t_ref[:, at] = (dot(etb, v) * (inv * scale) + dot(eb, vt) * inv).astype(BF16)
 
 
 VMEM = pl.BlockSpec(memory_space=pltpu.VMEM)
@@ -370,14 +390,13 @@
     pixels = rows * width
     tokens = frames * pixels // 4
 
-    me = lax.axis_index("clip")
-    gain = lax.dynamic_slice_in_dim(norm_gain, me * share, share, 0)[None, :]
-    embed_cut = lax.dynamic_slice_in_dim(embed_weight, me * share, share, 1)
-    time_cut = lax.dynamic_slice_in_dim(time_weight, me * share, share, 1)
+    gain, embed_cut, time_cut = norm_gain[None, :], embed_weight, time_weight
+    if share % LANES:
+        me = lax.axis_index("clip")
+        gain, embed_cut, time_cut = (
+            lax.dynamic_slice_in_dim(m, me * share, share, 1) for m in (gain, embed_weight, time_weight)
+        )
     weight = qkv_weight.transpose(1, 0, 2)
-    flow = flow_times.astype(F32) / TGRID
-    values, tangent = time_features(flow[:, 1:2], flow[:, 1:2] - flow[:, 0:1])
-    feats = jnp.concatenate([values, tangent, jnp.zeros((6, values.shape[1]), F32)], axis=0)
     features = clip_features.reshape(frames, pixels, depth_c)
     enc = enc_weight.transpose(0, 1, 2, 4, 3).reshape(27 * chans, depth_c)
     noise = noise_field[0].transpose(0, 1, 3, 2)
@@ -385,22 +404,28 @@
     source = np.stack(
         [((f * rows + 2 * i + p) * width + 2 * j + q).reshape(-1) for p in range(2) for q in range(2)]
     ).reshape(1, -1)
-    pick = (jnp.arange(frames * pixels, dtype=jnp.int32)[:, None] == source.astype(np.int32)).astype(BF16)
+    source = jnp.asarray(source.astype(np.int32))
     chunk = patch // clips
     dma = pltpu.SemaphoreType.DMA
     anywhere = pl.BlockSpec(memory_space=pl.ANY)
     edge = pltpu.VMEM((chans, frames * pixels), F32)
-    gathered, weights = pl.pallas_call(
+    x, xt, x_own, xt_own, weights = pl.pallas_call(
         functools.partial(front_kernel, (frames, width, chans, peers, clips)),
         out_shape=(
-            jax.ShapeDtypeStruct((2, peers * tokens, LANES), BF16),
+            jax.ShapeDtypeStruct((peers * tokens, LANES), BF16),
+            jax.ShapeDtypeStruct((peers * tokens, LANES), BF16),
+            jax.ShapeDtypeStruct((tokens, LANES), BF16),
+            jax.ShapeDtypeStruct((tokens, LANES), BF16),
             jax.ShapeDtypeStruct((peers, LANES, 3 * part), BF16),
         ),
-        in_specs=[VMEM] * 8 + [anywhere] * 3 + [VMEM],
-        out_specs=(VMEM, VMEM),
+        in_specs=[pl.BlockSpec(memory_space=pltpu.SMEM), VMEM] + [anywhere] * 9,
+        out_specs=(VMEM,) * 5,
         scratch_shapes=[
-            pltpu.VMEM(time_cut.shape, BF16), pltpu.VMEM(time_weight.shape, BF16), pltpu.VMEM(weight.shape, BF16), dma((3,)),
-            pltpu.VMEM((clips, 8, feats.shape[1]), F32), dma((clips - 1,)), dma((clips - 1,)),
+            pltpu.VMEM(weight.shape, BF16), pltpu.VMEM((patch, share), BF16), pltpu.VMEM((1, share), F32),
+            pltpu.VMEM((TFEAT, share), BF16), pltpu.VMEM(features.shape, BF16), pltpu.VMEM(enc.shape, BF16),
+            pltpu.VMEM(time_weight.shape, BF16), pltpu.VMEM(noise.shape, F32), pltpu.VMEM(embed_weight.shape, BF16),
+            dma((9,)), pltpu.VMEM((8, TFEAT), F32),
+            pltpu.VMEM((clips, 8, TFEAT), F32), dma((clips - 1,)), dma((clips - 1,)),
             edge, edge, edge, dma((2,)), dma((2,)),
             pltpu.VMEM((clips, chunk, 3 * part), F32), pltpu.VMEM((clips - 1, chunk, 3 * part), F32),
             pltpu.VMEM((clips, 2, 3 * part), F32), pltpu.VMEM((clips - 1, 2, 3 * part), F32),
@@ -412,11 +437,8 @@
         ],
         compiler_params=pltpu.CompilerParams(collective_id=0, has_side_effects=True),
         name="front",
-    )(features, enc, noise, flow[:, 1:2], feats, embed_weight, embed_cut, gain, time_cut, time_weight, weight, pick)
-    at = lax.axis_index("seq") * tokens
-    x_own = lax.dynamic_slice_in_dim(gathered[0], at, tokens, 0)
-    xt_own = lax.dynamic_slice_in_dim(gathered[1], at, tokens, 0)
-    output, output_t = attend(gathered[0], gathered[1], x_own, xt_own, weights, peers * part)
+    )(flow_times, source, weight, embed_cut, gain, time_cut, features, enc, time_weight, noise, embed_weight)
+    output, output_t = attend(x, xt, x_own, xt_own, weights, peers * part)
     return output[None], output_t[None]
 
 

time: 70.6 us -> 51.9 us (0.74)
  local copies, waits for them, and re-layouts: 8.23 us -> 0 us
  Pallas kernels: 56.1 us -> 51.1 us
  other arithmetic: 3.16 us -> 0 us
  between operations: 2.56 us -> 0.64 us
    dynamic_slice x5 -> x0, local copies, waits for them, and re-layouts: 5.22 us -> none  [the longest x1 1.72 us: local(): time_cut = lax.dynamic_slice_in_dim(time_weight, me * share, share, 1)]
    pallas_call x1, Pallas kernels: 35.7 us -> 31.4 us  [local(): pl.pallas_call(functools.partial(front_kernel, (frames, width, chans, pee...]
    slice x2 -> x0, local copies, waits for them, and re-layouts: 2.33 us -> none  [the longest x1 1.74 us: local(): gathered[1]]
    convert_element_type x1 -> x0, other arithmetic: 1.61 us -> none  [local(): (jnp.arange(frames * pixels, dtype=jnp.int32)[:, None] == source.astype(n...]
where the time goes in v2:
time: 51.9 us; the launch traced here: 51.7 us
  Pallas kernels  51.1 us (98%)
  between operations  0.64 us (1%)
    pallas_call x1, Pallas kernels, local(): pl.pallas_call(functools.partial(front_kernel, (frames, width, chans, pee...  31.4 us
    pallas_call x1, Pallas kernels, attend(): pl.pallas_call(functools.partial(attend_kernel, per), grid=(peers * count...  19.7 us

profile of v2, /device:TPU:0, one launch (start us, length us, event | category | flops | bytes accessed | tf_op | source)
XLA Modules:
  0.0 51.7 jit_solution(17894914120474681803)
XLA Ops:
  0.6 31.4 %front.1 = (bf16[512,128]{1,0:T(8,128)(2,1)}, bf16[512,128]{1,0:T(8,128)(2,1)}, bf16[128,128]{1,0:T(8,128)(2,1)}, bf16[128,128]{1,0:T(8,128)(2,1)}, bf16[4,128,2304]{2,1,0:T(8,128)(2,1)}) custom-call(s32[1,2]{1,0:T(1,128)} %flow_ref.1, s32[1,512]{1,0:T(1,128)} %constant.2.clone.source_ref, bf16[3,640,768]{2,1,0:T(8,128)(2,1)} %bitcast.11, ...), custom_call_target="tpu_custom_call" | custom-call | tf_op jit(solution)/shard_map/front/pallas_call | solution.py:412
  32.0 19.7 %attend.1 = (bf16[128,3072]{1,0:T(8,128)(2,1)}, bf16[128,3072]{1,0:T(8,128)(2,1)}) custom-call(bf16[512,128]{1,0:T(8,128)(2,1)} %get-tuple-element.9.x_ref, bf16[512,128]{1,0:T(8,128)(2,1)} %get-tuple-element.10.xt_ref, bf16[128,128]{1,0:T(8,128)(2,1)} %get-tuple-element.11.xo_ref, bf16[128,128]{1,0:T(8,128)(2,1)} %get-tuple-element.12.xto_ref, ...), custom_call_target="tpu_custom_call" | custom-call | tf_op jit(solution)/shard_map/attend/pallas_call | solution.py:373

commit v3 on v2

--- a/solution.py
+++ b/solution.py
@@ -121,7 +121,7 @@
 def front_kernel(
     dims,
     flow_ref, source_ref, w_hbm, ecut_hbm, gcut_hbm, tcut_hbm, f_hbm, enc_hbm, time_hbm, noise_hbm, embed_hbm,
-    x_out, xt_out, x_own, xt_own, m_out,
+    x_out, x_own, m_out,
     w_ref, ecut_ref, gcut_ref, tcut_ref, f_ref, enc_ref, time_ref, noise_ref, embed_ref, load_sem, feats_ref,
     feats_buf, feats_send, feats_recv,
     edge_buf, before_buf, after_buf, edge_send, edge_recv,
@@ -305,12 +305,12 @@
         c_in.append(push(g_buf.at[src], g_buf.at[src], c_ss.at[k + 1], c_rs.at[k + 1], mate))
     for copy in bt_in + x_in + c_in:
         copy.wait_recv()
-    x_own[...] = x_buf[seq, 0]
-    xt_own[...] = x_buf[seq, 1]
     tokens = x_buf.shape[2]
+    x_own[:tokens] = x_buf[seq, 0]
+    x_own[tokens:] = x_buf[seq, 1]
     for p in range(peers):
         x_out[p * tokens : (p + 1) * tokens] = x_buf[p, 0]
-        xt_out[p * tokens : (p + 1) * tokens] = x_buf[p, 1]
+        x_out[(peers + p) * tokens : (peers + p + 1) * tokens] = x_buf[p, 1]
         for c in range(clips):
             m_out[p, c * chunk : (c + 1) * chunk] = g_buf[c, p]
         hi = tau_buf[p].astype(BF16).astype(F32)
@@ -333,39 +333,40 @@
         to_last.wait_send()
 
 
-def attend_kernel(per, x_ref, xt_ref, xo_ref, xto_ref, q_ref, k_ref, v_ref, out_ref, out_t_ref):
+def attend_kernel(per, x_ref, own_ref, q_ref, k_ref, v_ref, out_ref, out_t_ref):
     scale = HD ** (-0.5)
-    wq, wk, wv = q_ref[0], k_ref[0], v_ref[0]
-
-    def project(rows_ref, weight):
-        return dot(rows_ref[...], weight).astype(BF16)
-
-    keys, keys_t = project(x_ref, wk), project(xt_ref, wk)
-    vals, vals_t = project(x_ref, wv), project(xt_ref, wv)
-    query, query_t = project(xo_ref, wq), project(xto_ref, wq)
+    total, tokens = x_ref.shape[0] // 2, own_ref.shape[0] // 2
+    keys = dot(x_ref[...], k_ref[0]).astype(BF16)
+    vals = dot(x_ref[...], v_ref[0]).astype(BF16)
+    query = dot(own_ref[...], q_ref[0]).astype(BF16)
+    zero = jnp.zeros((tokens, HD), BF16)
     for h in range(per):
         at = slice(h * HD, (h + 1) * HD)
-        q, qt, k, kt, v, vt = (m[:, at] for m in (query, query_t, keys, keys_t, vals, vals_t))
-        scores = dot_nt(q, k)
-        score_t = dot_nt(jnp.concatenate([qt, q], axis=1), jnp.concatenate([k, kt], axis=1))
+        q, qt = query[:tokens, at], query[tokens:, at]
+        left = jnp.concatenate(
+            [jnp.concatenate([q, zero], axis=1), jnp.concatenate([qt, q], axis=1)], axis=0
+        )
+        both = dot_nt(left, jnp.concatenate([keys[:total, at], keys[total:, at]], axis=1))
+        scores, score_t = both[:tokens], both[tokens:]
         expo = jnp.exp((scores - jnp.max(scores, axis=1, keepdims=True)) * scale)
         inv = 1.0 / jnp.sum(expo, axis=1, keepdims=True)
         mean = jnp.sum(expo * score_t, axis=1, keepdims=True) * inv
-        eb, etb = expo.astype(BF16), (expo * (score_t - mean)).astype(BF16)
-        out_ref[:, at] = (dot(eb, v) * inv).astype(BF16)
-        out_t_ref[:, at] = (dot(etb, v) * (inv * scale) + dot(eb, vt) * inv).astype(BF16)
+        left = jnp.concatenate([expo.astype(BF16), (expo * (score_t - mean)).astype(BF16)], axis=0)
+        both = dot(left, jnp.concatenate([vals[:total, at], vals[total:, at]], axis=1))
+        out_ref[:, at] = (both[:tokens, :HD] * inv).astype(BF16)
+        out_t_ref[:, at] = (both[tokens:, :HD] * (inv * scale) + both[:tokens, HD:] * inv).astype(BF16)
 
 
 VMEM = pl.BlockSpec(memory_space=pltpu.VMEM)
 
 
-def attend(rows, rows_t, own, own_t, weights, inner):
+def attend(rows, own, weights, inner):
     peers, depth, width = weights.shape
     part = width // 3
-    per = 2 if (part // HD) % 2 == 0 else 1
+    per = part // HD
     block = per * HD
     count = part // block
-    tokens, total = own.shape[0], rows.shape[0]
+    tokens, total = own.shape[0] // 2, rows.shape[0]
     whole = lambda n: pl.BlockSpec((n, LANES), lambda i: (0, 0))
     spec = lambda g: pl.BlockSpec((1, depth, block), lambda i: (i // count, 0, g * count + i % count))
     out = pl.BlockSpec((tokens, block), lambda i: (0, i))
@@ -374,10 +375,10 @@
         functools.partial(attend_kernel, per),
         grid=(peers * count,),
         out_shape=(shape, shape),
-        in_specs=[whole(total), whole(total), whole(tokens), whole(tokens), spec(0), spec(1), spec(2)],
+        in_specs=[whole(total), whole(2 * tokens), spec(0), spec(1), spec(2)],
         out_specs=(out, out),
         name="attend",
-    )(rows, rows_t, own, own_t, weights, weights, weights)
+    )(rows, own, weights, weights, weights)
 
 
 def local(clip_features, enc_weight, noise_field, flow_times, embed_weight, time_weight, norm_gain, qkv_weight):
@@ -409,17 +410,15 @@
     dma = pltpu.SemaphoreType.DMA
     anywhere = pl.BlockSpec(memory_space=pl.ANY)
     edge = pltpu.VMEM((chans, frames * pixels), F32)
-    x, xt, x_own, xt_own, weights = pl.pallas_call(
+    x, x_own, weights = pl.pallas_call(
         functools.partial(front_kernel, (frames, width, chans, peers, clips)),
         out_shape=(
-            jax.ShapeDtypeStruct((peers * tokens, LANES), BF16),
-            jax.ShapeDtypeStruct((peers * tokens, LANES), BF16),
-            jax.ShapeDtypeStruct((tokens, LANES), BF16),
-            jax.ShapeDtypeStruct((tokens, LANES), BF16),
+            jax.ShapeDtypeStruct((2 * peers * tokens, LANES), BF16),
+            jax.ShapeDtypeStruct((2 * tokens, LANES), BF16),
             jax.ShapeDtypeStruct((peers, LANES, 3 * part), BF16),
         ),
         in_specs=[pl.BlockSpec(memory_space=pltpu.SMEM), VMEM] + [anywhere] * 9,
-        out_specs=(VMEM,) * 5,
+        out_specs=(VMEM,) * 3,
         scratch_shapes=[
             pltpu.VMEM(weight.shape, BF16), pltpu.VMEM((patch, share), BF16), pltpu.VMEM((1, share), F32),
             pltpu.VMEM((TFEAT, share), BF16), pltpu.VMEM(features.shape, BF16), pltpu.VMEM(enc.shape, BF16),
@@ -438,7 +437,7 @@
         compiler_params=pltpu.CompilerParams(collective_id=0, has_side_effects=True),
         name="front",
     )(flow_times, source, weight, embed_cut, gain, time_cut, features, enc, time_weight, noise, embed_weight)
-    output, output_t = attend(x, xt, x_own, xt_own, weights, peers * part)
+    output, output_t = attend(x, x_own, weights, peers * part)
     return output[None], output_t[None]
 
 

time: 51.9 us -> 44 us (0.85)
  Pallas kernels: 51.1 us -> 43.2 us
    pallas_call x1, Pallas kernels: 19.7 us -> 11.8 us  [attend(): pl.pallas_call(functools.partial(attend_kernel, per), grid=(peers * count...]
where the time goes in v3:
time: 44 us; the launch traced here: 43.8 us
  Pallas kernels  43.2 us (98%)
  between operations  0.64 us (1%)
    pallas_call x1, Pallas kernels, local(): pl.pallas_call(functools.partial(front_kernel, (frames, width, chans, pee...  31.4 us
    pallas_call x1, Pallas kernels, attend(): pl.pallas_call(functools.partial(attend_kernel, per), grid=(peers * count...  11.8 us

profile of v3, /device:TPU:0, one launch (start us, length us, event | category | flops | bytes accessed | tf_op | source)
XLA Modules:
  0.0 43.8 jit_solution(11952814929416335453)
XLA Ops:
  0.6 31.4 %front.1 = (bf16[1024,128]{1,0:T(8,128)(2,1)}, bf16[256,128]{1,0:T(8,128)(2,1)}, bf16[4,128,2304]{2,1,0:T(8,128)(2,1)}) custom-call(s32[1,2]{1,0:T(1,128)} %flow_ref.1, s32[1,512]{1,0:T(1,128)} %constant.2.clone.source_ref, bf16[3,640,768]{2,1,0:T(8,128)(2,1)} %bitcast.11, bf16[64,5120]{1,0:T(8,128)(2,1)} %embed_hbm.1, f32[1,5120]{1,0:T(1,128)} %bitcast.15, ...), custom_call_target="tpu_custom_call" | custom-call | tf_op jit(solution)/shard_map/front/pallas_call | solution.py:413
  32.0 11.8 %attend.1 = (bf16[128,3072]{1,0:T(8,128)(2,1)}, bf16[128,3072]{1,0:T(8,128)(2,1)}) custom-call(bf16[1024,128]{1,0:T(8,128)(2,1)} %get-tuple-element.7.x_ref, bf16[256,128]{1,0:T(8,128)(2,1)} %get-tuple-element.8.own_ref, bf16[4,128,2304]{2,1,0:T(8,128)(2,1)} %get-tuple-element.9.q_ref.k_ref.v_ref, bf16[4,128,2304]{2,1,0:T(8,128)(2,1)} %get-tuple-element.9.q_ref.k_ref.v_ref, ...), custom_call_target="tpu_custom_call" | custom-call | tf_op jit(solution)/shard_map/attend/pallas_call | solution.py:374

commit v4 on v3

--- a/solution.py
+++ b/solution.py
@@ -194,7 +194,7 @@
         both = dot(left, w_ref[i])
         both = both[:patch] + both[patch:]
         for c in range(clips):
-            e_send[c, :, i * part : (i + 1) * part] = both[c * chunk : (c + 1) * chunk]
+            e_send[c, :, i * part : (i + 1) * part] = both[c * chunk : (c + 1) * chunk].astype(BF16)
     e_in = [
         push(e_send.at[lax.rem(clip + k + 1, clips)], e_recv.at[k], e_ss.at[k], e_rs.at[k], who)
         for k, who in enumerate(on_clip)
@@ -251,9 +251,9 @@
 
     for copy in e_in:
         copy.wait_recv()
-    total = e_send[clip]
+    total = e_send[clip].astype(F32)
     for k in range(clips - 1):
-        total = total + e_recv[k]
+        total = total + e_recv[k].astype(F32)
     g_buf[clip, seq] = total.astype(BF16)
     b_in = [
         push(g_buf.at[clip, seq], g_buf.at[clip, seq], b_ss.at[k], b_rs.at[k], who) for k, who in enumerate(on_seq)
@@ -426,7 +426,7 @@
             dma((9,)), pltpu.VMEM((8, TFEAT), F32),
             pltpu.VMEM((clips, 8, TFEAT), F32), dma((clips - 1,)), dma((clips - 1,)),
             edge, edge, edge, dma((2,)), dma((2,)),
-            pltpu.VMEM((clips, chunk, 3 * part), F32), pltpu.VMEM((clips - 1, chunk, 3 * part), F32),
+            pltpu.VMEM((clips, chunk, 3 * part), BF16), pltpu.VMEM((clips - 1, chunk, 3 * part), BF16),
             pltpu.VMEM((clips, 2, 3 * part), F32), pltpu.VMEM((clips - 1, 2, 3 * part), F32),
             dma((clips - 1,)), dma((clips - 1,)), dma((clips - 1,)), dma((clips - 1,)),
             pltpu.VMEM((peers, 2, tokens, LANES), BF16), dma((peers - 1,)), dma((peers - 1,)),

time: 44 us -> 41.7 us (0.948)
  Pallas kernels: 43.2 us -> 40.9 us
    pallas_call x1, Pallas kernels: 31.4 us -> 29.1 us  [local(): pl.pallas_call(functools.partial(front_kernel, (frames, width, chans, pee...]
where the time goes in v4:
time: 41.7 us; the launch traced here: 41.5 us
  Pallas kernels  40.9 us (98%)
  between operations  0.64 us (2%)
    pallas_call x1, Pallas kernels, local(): pl.pallas_call(functools.partial(front_kernel, (frames, width, chans, pee...  29.1 us
    pallas_call x1, Pallas kernels, attend(): pl.pallas_call(functools.partial(attend_kernel, per), grid=(peers * count...  11.8 us

profile of v4, /device:TPU:0, one launch (start us, length us, event | category | flops | bytes accessed | tf_op | source)
XLA Modules:
  0.0 41.5 jit_solution(17639485365107345049)
XLA Ops:
  0.6 29.1 %front.1 = (bf16[1024,128]{1,0:T(8,128)(2,1)}, bf16[256,128]{1,0:T(8,128)(2,1)}, bf16[4,128,2304]{2,1,0:T(8,128)(2,1)}) custom-call(s32[1,2]{1,0:T(1,128)} %flow_ref.1, s32[1,512]{1,0:T(1,128)} %constant.2.clone.source_ref, bf16[3,640,768]{2,1,0:T(8,128)(2,1)} %bitcast.11, bf16[64,5120]{1,0:T(8,128)(2,1)} %embed_hbm.1, f32[1,5120]{1,0:T(1,128)} %bitcast.15, ...), custom_call_target="tpu_custom_call" | custom-call | tf_op jit(solution)/shard_map/front/pallas_call | solution.py:413
  29.7 11.8 %attend.1 = (bf16[128,3072]{1,0:T(8,128)(2,1)}, bf16[128,3072]{1,0:T(8,128)(2,1)}) custom-call(bf16[1024,128]{1,0:T(8,128)(2,1)} %get-tuple-element.7.x_ref, bf16[256,128]{1,0:T(8,128)(2,1)} %get-tuple-element.8.own_ref, bf16[4,128,2304]{2,1,0:T(8,128)(2,1)} %get-tuple-element.9.q_ref.k_ref.v_ref, bf16[4,128,2304]{2,1,0:T(8,128)(2,1)} %get-tuple-element.9.q_ref.k_ref.v_ref, ...), custom_call_target="tpu_custom_call" | custom-call | tf_op jit(solution)/shard_map/attend/pallas_call | solution.py:374
